TPU v7x, 256 devices: a whole 4x4x8 slice. The times are simulated.
256 devices in a mesh: dp: 16 (over z, x_lo), seq: 16 (over y, x_hi, core).
Axes of the slice: x: 4 (x_hi: 2, x_lo: 2; x = x_hi * 2 + x_lo), y: 4, z: 8, core: 2. Of those that a mesh axis runs over, the one named last changes fastest.
Arguments:
- frames: bfloat16 [16, 4096, 1536], P('dp', 'seq'), may hold values from -0.29882812 to 0.29882812
- segment_ids: int32 [16, 4096], P('dp', 'seq'), may hold values from 0 to 11, never falling along the last dimension, each value on 1 to 3072 neighbouring positions
- ln_attn_gain: float32 [1536], replicated, may hold values from 0.25 to 1.75
- w_qkv: bfloat16 [1536, 2304], P('dp'), as said below
- w_out: bfloat16 [768, 1536], P('dp'), may hold values from -0.21875 to 0.21875
- ln_conv_gain: float32 [1536], replicated, may hold values from 0.25 to 1.75
- w_glu: bfloat16 [1536, 3072], P('dp'), may hold values from -0.15625 to 0.15625
- dw_kernel: float32 [32, 1536], replicated, may hold values from -1 to 1
- ln_mid_gain: float32 [1536], replicated, may hold values from 0.25 to 1.75
Outputs:
- block_out: bfloat16 [16, 4096, 1536], P('dp', 'seq')
Inputs may be any that keep to these rules, and one draw needn't show every extreme that they name: `segment_ids`: within each stream the ids start at 0 and never fall; each utterance has 1 to 3072 frames and one has exactly 3072. `w_qkv`: a projection matrix with independent entries.
All inputs are finite; a program needn't handle non-finite values.
Results may differ from a plain program's by a relative error of at most 0.025.
The roundings to bfloat16 on the way count: a program that leaves them out, or rounds other values in their place, can miss the bound.
Values may be sent and summed in bfloat16 or wider, within the bound.
No kernel may reach another device: no remote copies, remote signals or barrier semaphores. Data moves between devices by JAX's collectives and lax.ppermute only.
A program may use at most 192 MiB of HBM per device.

v0:
```python
import math
import jax
import jax.numpy as jnp
from jax import lax
from jax.sharding import PartitionSpec as P

D = 1536
HEADS = 12
HD = 64
CONV_K = 32


def with_halo(block, sides, width):
    for axis, dim in sides:
        count = lax.axis_size(axis)
        forward = [(i, i + 1) for i in range(count - 1)]
        backward = [(target, source) for source, target in forward]
        low = lax.ppermute(
            lax.slice_in_dim(block, block.shape[dim] - width, None, axis=dim), axis, forward
        )
        high = lax.ppermute(lax.slice_in_dim(block, 0, width, axis=dim), axis, backward)
        block = jnp.concatenate([low, block, high], axis=dim)
    return block


def layer_norm(values, gain):
    values = values.astype(jnp.float32)
    centre = jnp.mean(values, -1, keepdims=True)
    spread = jnp.mean((values - centre) ** 2, -1, keepdims=True)
    return (values - centre) * lax.rsqrt(spread + 1e-05) * gain


def add_rows(left, block_rows):
    return jnp.dot(left, block_rows, preferred_element_type=jnp.float32)


def body(
    frames, segment_ids, ln_attn_gain, w_qkv, w_out, ln_conv_gain, w_glu, dw_kernel, ln_mid_gain
):
    width = HEADS * HD
    local = frames[0]
    frame_count = local.shape[0]
    local_segs = segment_ids[0]
    shard_index = lax.axis_index("seq")
    first_frame = shard_index * frame_count
    all_segs = lax.all_gather(segment_ids, "seq", axis=1, tiled=True)[0]
    normed = layer_norm(local, ln_attn_gain).astype(jnp.bfloat16)
    projected = add_rows(normed, lax.all_gather(w_qkv, "dp", axis=0, tiled=True))
    projected = projected.astype(jnp.bfloat16)
    queries = projected[:, :width].reshape(frame_count, HEADS, HD)
    keys_local = projected[:, width : 2 * width]
    values_local = projected[:, 2 * width :]
    inverse_root = 1.0 / math.sqrt(HD)
    keys_part = lax.all_gather(keys_local, "seq", axis=0, tiled=True)
    values_part = lax.all_gather(values_local, "seq", axis=0, tiled=True)
    rows = keys_part.shape[0]
    running = jnp.full((HEADS, frame_count), -1e30, jnp.float32)
    scores = (
        jnp.einsum(
            "qhd,khd->hqk",
            queries,
            keys_part.reshape(rows, HEADS, HD),
            preferred_element_type=jnp.float32,
        )
        * inverse_root
    )
    same_seg = (local_segs[:, None] == all_segs[None, :])[None]
    scores = jnp.where(same_seg, scores, -1e30)
    newest = jnp.maximum(running, jnp.max(scores, -1))
    raised = jnp.where(same_seg, jnp.exp(scores - newest[:, :, None]), 0.0)
    totals = jnp.sum(raised, -1)
    product = jnp.einsum(
        "hqk,khd->qhd",
        raised.astype(jnp.bfloat16),
        values_part.reshape(rows, HEADS, HD),
        preferred_element_type=jnp.float32,
    )
    summed = product
    running, totals, summed = (newest, totals, summed.reshape(frame_count, width))
    attended = (
        (summed.reshape(frame_count, HEADS, HD) / jnp.transpose(totals)[:, :, None])
        .reshape(frame_count, width)
        .astype(jnp.bfloat16)
    )
    attn = add_rows(attended, lax.all_gather(w_out, "dp", axis=0, tiled=True))
    resid = (local.astype(jnp.float32) + attn).astype(jnp.bfloat16)
    glu_in = layer_norm(resid, ln_conv_gain).astype(jnp.bfloat16)
    glu_out = add_rows(glu_in, lax.all_gather(w_glu, "dp", axis=0, tiled=True))
    gated = (glu_out[:, :D] * jax.nn.sigmoid(glu_out[:, D:])).astype(jnp.bfloat16)
    half_taps = CONV_K // 2
    widened = with_halo(gated, (("seq", 0),), half_taps)
    padded_segs = jnp.pad(all_segs, (half_taps, half_taps), constant_values=-1)
    rim_segs = lax.dynamic_slice_in_dim(padded_segs, first_frame, frame_count + 2 * half_taps)
    conv = jnp.zeros((frame_count, D), jnp.float32)
    for tap_index in range(CONV_K):
        keep = (rim_segs[tap_index : tap_index + frame_count] == local_segs)[:, None]
        shifted = widened[tap_index : tap_index + frame_count].astype(jnp.float32)
        conv = conv + jnp.where(keep, shifted * dw_kernel[tap_index], 0.0)
    middle = layer_norm(conv, ln_mid_gain)
    result = (resid.astype(jnp.float32) + middle * jax.nn.sigmoid(middle)).astype(jnp.bfloat16)
    return result[None]


def solution(mesh):
    return jax.shard_map(
        body,
        mesh=mesh,
        in_specs=(
            P("dp", "seq", None),
            P("dp", "seq"),
            P(),
            P("dp", None),
            P("dp", None),
            P(),
            P("dp", None),
            P(),
            P(),
        ),
        out_specs=P("dp", "seq", None),
        check_vma=False,
    )
```

profile of v0, /device:TPU:39, one launch (start us, length us, event | category | flops | bytes accessed | tf_op | source)
XLA Modules:
  0.0 635.7 jit_solution(8516103408520678854)
XLA Ops:
  6.5 0.0 copy-start
  6.5 0.0 copy-start.4
  6.5 0.0 all-gather.6.cloned.1.call-start
  6.5 0.7 all-gather.6.cloned.1.call-update
  7.3 0.0 all-gather.10.cloned.1.call-start
  7.3 1.3 convert_reduce_fusion
  8.6 0.0 copy-done
  8.6 0.3 fusion.11
  9.0 159.5 %all-gather.6.cloned.1.call-done = bf16[1536,2304]{1,0:T(8,128)(2,1)} async-done(((bf16[96,2304]{1,0:T(8,128)(2,1)}), bf16[1536,2304]{1,0:T(8,128)(2,1)}) %all-gather.6.cloned.1.call-update) | async-done | bytes 7077904 | tf_op jit(solution)/shard_map/all_gather | solution.py:48
  168.5 0.0 copy-done.4
  168.5 5.1 convolution_convert_fusion
  173.6 0.0 copy-start.2
  173.6 0.0 copy-start.1
  173.6 1.0 fusion.70
  174.6 0.0 all-gather.10.cloned.1.call-update
  174.6 0.0 all-gather.8.cloned.1.call-start
  174.7 0.7 all-gather.8.cloned.1.call-update
  175.4 0.0 all-gather.12.cloned.1.call-start
  175.4 0.5 all-gather.12.cloned.1.call-update
  175.9 0.0 all-gather.14.cloned.1.call-start
  176.0 0.5 all-gather.14.cloned.1.call-update
  176.5 0.0 copy-done.2
  176.6 22.1 %all_gather.22 = s32[1,4096]{1,0:T(1,128)S(1)} all-gather(s32[1,256]{1,0:T(1,128)S(1)} %copy-done.2), channel_id=1, replica_groups=mesh['dp'=16,'seq'=16] {'seq'}, dimensions={1}, use_global_device_ids=true | all-gather | bytes 17408 | tf_op jit(solution)/shard_map/all_gather | solution.py:46
  198.6 0.1 pad_dynamic-slice_fusion
  198.7 0.0 copy-done.1
  198.7 0.3 slice_reduce_fusion.31
  199.0 0.1 slice_compare_fusion.30
  199.1 0.1 slice_compare_fusion.31
  199.2 0.6 broadcast_compare_fusion
  199.9 0.2 copy.14
  200.0 43.1 %all-gather.10.cloned.1.call-done = bf16[4096,768]{1,0:T(8,128)(2,1)} async-done(((bf16[256,768]{1,0:T(8,128)(2,1)}), bf16[4096,768]{1,0:T(8,128)(2,1)}) %all-gather.10.cloned.1.call-update) | async-done | bytes 6291472 | tf_op jit(solution)/shard_map/all_gather | solution.py:54
  243.1 8.6 %copy.15 = bf16[4096,768]{0,1:T(8,128)(2,1)} copy(bf16[4096,768]{1,0:T(8,128)(2,1)} %all-gather.10.cloned.1.call-done) | data formatting | bytes 12582912 | tf_op jit(solution)/shard_map/all_gather | solution.py:54
  251.7 61.2 %all-gather.8.cloned.1.call-done = bf16[4096,768]{1,0:T(8,128)(2,1)} async-done(((bf16[256,768]{1,0:T(8,128)(2,1)}), bf16[4096,768]{1,0:T(8,128)(2,1)}) %all-gather.8.cloned.1.call-update) | async-done | bytes 6291472 | tf_op jit(solution)/shard_map/all_gather | solution.py:55
  312.9 8.7 %copy.13 = bf16[4096,768]{0,1:T(8,128)(2,1)} copy(bf16[4096,768]{1,0:T(8,128)(2,1)} %all-gather.8.cloned.1.call-done) | data formatting | bytes 12582912 | tf_op jit(solution)/shard_map/all_gather | solution.py:55
  321.6 23.4 %fusion = (f32[12,256]{1,0:T(8,128)S(1)}, f32[12,256,4096]{2,1,0:T(8,128)}) fusion(pred[256,4096]{1,0:T(8,128)(4,1)S(1)} %broadcast_compare_fusion, bf16[256,12,64]{0,2,1:T(8,128)(2,1)S(1)} %bitcast.41, bf16[4096,12,64]{0,2,1:T(8,128)(2,1)} %bitcast.39), kind=kOutput, calls=%fused_computation.2 | convolution fusion | flops 1648358400 | bytes 58077184 | tf_op jit(solution)/shard_map/qhd,khd->hqk/dot_general | solution.py:59
  345.0 23.5 %fusion.1 = f32[12,256]{1,0:T(8,128)S(1)} fusion(f32[12,256,4096]{2,1,0:T(8,128)} %get-tuple-element.77, f32[12,256]{1,0:T(8,128)S(1)} %broadcast_maximum_fusion, pred[256,4096]{1,0:T(8,128)(4,1)S(1)} %broadcast_compare_fusion), kind=kLoop, calls=%fused_computation.3 | loop fusion | flops 62911488 | bytes 51404800 | tf_op jit(solution)/shard_map/reduce_sum | solution.py:71
  368.5 21.7 %fusion.25 = bf16[256,12,64]{0,2,1:T(8,128)(2,1)S(1)} fusion(bf16[4096,12,64]{0,2,1:T(8,128)(2,1)} %bitcast.40, f32[12,256,4096]{2,1,0:T(8,128)} %get-tuple-element.77, f32[12,256]{1,0:T(8,128)S(1)} %broadcast_maximum_fusion, pred[256,4096]{1,0:T(8,128)(4,1)S(1)} %broadcast_compare_fusion, f32[256,12]{0,1:T(8,128)S(1)} %bitcast.45), kind=kOutput, calls=%fused_computation.62 | convolution fusion | flops 1673920512 | bytes 58089472 | tf_op jit(solution)/shard_map/hqk,khd->qhd/dot_general | solution.py:72
  390.2 0.0 all-gather.12.cloned.1.call-done
  390.2 2.5 fusion.72
  392.8 0.0 copy-start.5
  392.8 0.3 multiply_reduce_fusion.1
  393.1 199.7 %all-gather.14.cloned.1.call-done = bf16[1536,3072]{1,0:T(8,128)(2,1)} async-done(((bf16[96,3072]{1,0:T(8,128)(2,1)}), bf16[1536,3072]{1,0:T(8,128)(2,1)}) %all-gather.14.cloned.1.call-update) | async-done | bytes 9437200 | tf_op jit(solution)/shard_map/all_gather | solution.py:88
  592.8 0.0 copy-done.5
  592.8 5.3 fusion.28
  598.0 0.4 fusion.18
  598.5 4.7 collective-permute-start
  603.2 1.9 collective-permute-start.1
  605.1 0.2 slice_reduce_fusion.30
  605.3 0.0 collective-permute-done
  605.4 5.7 collective-permute-done.1
  611.0 0.0 copy-start.3
  611.0 16.3 %fusion.69 = (f32[256]{0:T(256)S(1)}, f32[256,1536]{1,0:T(8,128)S(1)}) fusion(f32[1536]{0:T(1024)S(1)} %get-tuple-element.35, bf16[16,1536]{1,0:T(8,128)(2,1)S(1)} %collective-permute-done.1, bf16[256,1536]{1,0:T(8,128)(2,1)S(1)} %fusion.18, pred[256]{0:T(512)(128)(4,1)S(1)} %get-tuple-element.45, f32[1536]{0:T(1024)S(1)} %get-tuple-element.36, ...), kind=kLoop, calls=%fused_computation.195 | loop fusion | flops 86900480 | bytes 2663424 | tf_op jit(solution)/shard_map/reduce_sum | solution.py:28
  627.3 0.3 multiply_reduce_fusion
  627.6 0.0 copy-done.3
  627.6 1.5 fusion.65
  (8 shorter events, 0.1 us)
Async XLA Ops:
  6.5 2.1 copy-start
  6.5 161.9 %copy-start.4 = (f32[1536]{0:T(1024)S(1)}, f32[1536]{0:T(1024)}, u32[]{:S(2)}) copy-start(f32[1536]{0:T(1024)} %param.11) | copy-start | bytes 18436
  6.5 161.9 %all-gather.6.cloned.1.call-start = ((), (), s32[]{:S(2)}) async-start(), calls=%async_computation | async-start | bytes 7520256 | tf_op jit(solution)/shard_map/all_gather | solution.py:48
  7.3 235.9 %all-gather.10.cloned.1.call-start = ((), (), s32[]{:S(2)}) async-start(), calls=%async_computation.2 | async-start | bytes 6684672 | tf_op jit(solution)/shard_map/all_gather | solution.py:54
  173.6 2.9 copy-start.2
  173.6 25.1 %copy-start.1 = (f32[32,1536]{1,0:T(8,128)S(1)}, f32[32,1536]{1,0:T(8,128)}, u32[]{:S(2)}) copy-start(f32[32,1536]{1,0:T(8,128)} %param.16) | copy-start | bytes 589828
  174.6 138.3 %all-gather.8.cloned.1.call-start = ((), (), s32[]{:S(2)}) async-start(), calls=%async_computation.1 | async-start | bytes 6684672 | tf_op jit(solution)/shard_map/all_gather | solution.py:55
  175.4 214.9 %all-gather.12.cloned.1.call-start = ((), (), s32[]{:S(2)}) async-start(), calls=%async_computation.3 | async-start | bytes 2506752 | tf_op jit(solution)/shard_map/all_gather | solution.py:85
  175.9 416.8 %all-gather.14.cloned.1.call-start = ((), (), s32[]{:S(2)}) async-start(), calls=%async_computation.4 | async-start | bytes 10027008 | tf_op jit(solution)/shard_map/all_gather | solution.py:88
  392.8 200.0 %copy-start.5 = (f32[1536]{0:T(1024)S(1)}, f32[1536]{0:T(1024)}, u32[]{:S(2)}) copy-start(f32[1536]{0:T(1024)} %param.14) | copy-start | bytes 18436
  598.5 6.9 %collective-permute-start = (bf16[16,1536]{1,0:T(8,128)(2,1)S(1)}, bf16[16,1536]{1,0:T(8,128)(2,1)S(1)}, u32[]{:S(2)}, u32[]{:S(2)}) collective-permute-start(bf16[16,1536]{1,0:T(8,128)(2,1)S(1)} %get-tuple-element.42), channel_id=1, source_target_pairs={{0,1},{1,2},{2,3},{3,4},{4,5},{5,6},{6,7},{7,8},{8,9},{9,10},{10,1... | collective-permute-start | bytes 147464 | tf_op jit(solution)/shard_map/ppermute | solution.py:18
  603.2 7.8 %collective-permute-start.1 = (bf16[16,1536]{1,0:T(8,128)(2,1)S(1)}, bf16[16,1536]{1,0:T(8,128)(2,1)S(1)}, u32[]{:S(2)}, u32[]{:S(2)}) collective-permute-start(bf16[16,1536]{1,0:T(8,128)(2,1)S(1)} %get-tuple-element.43), channel_id=1, source_target_pairs={{1,0},{2,1},{3,2},{4,3},{5,4},{6,5},{7,6},{8,7},{9,8},{10,9},{11,1... | collective-permute-start | bytes 147464 | tf_op jit(solution)/shard_map/ppermute | solution.py:21
  611.0 16.6 %copy-start.3 = (f32[1536]{0:T(1024)S(1)}, f32[1536]{0:T(1024)}, u32[]{:S(2)}) copy-start(f32[1536]{0:T(1024)} %param.17) | copy-start | bytes 18436
Sparse Core Ops, SparseCore 0:
  9.1 159.2 all-gather.5
  174.8 68.3 all-gather.9
  245.9 66.9 all-gather.7
  314.6 64.0 all-gather.11
  380.3 212.4 all-gather.13
where the time goes:
time: 637 us; the launch traced here: 636 us
  waiting for transfers between devices  472 us (74%)
  matrix products  58 us (9%)
  other arithmetic  44.8 us (7%)
  blocking collectives  22.1 us (3%)
  local copies, waits for them, and re-layouts  19.1 us (3%)
  between operations  13.3 us (2%)
  starting transfers between devices  6.79 us (1%)
    all_gather x1, waiting for transfers between devices, body(): glu_out = add_rows(glu_in, lax.all_gather(w_glu, 'dp', axis=0, tiled=True))  200 us
    all_gather x1, waiting for transfers between devices, body(): lax.all_gather(w_qkv, 'dp', axis=0, tiled=True)  159 us
    all_gather x1, waiting for transfers between devices, body(): values_part = lax.all_gather(values_local, 'seq', axis=0, tiled=True)  61.2 us
    all_gather x1, waiting for transfers between devices, body(): keys_part = lax.all_gather(keys_local, 'seq', axis=0, tiled=True)  43.1 us
    reduce_sum x1, other arithmetic, body(): totals = jnp.sum(raised, -1)  23.5 us
    dot_general x1, matrix products, body(): jnp.einsum('qhd,khd->hqk', queries, keys_part.reshape(rows, HEADS, HD), p...  23.4 us
    all_gather x1, blocking collectives, body(): all_segs = lax.all_gather(segment_ids, 'seq', axis=1, tiled=True)[0]  22.1 us
    dot_general x1, matrix products, body(): jnp.einsum('hqk,khd->qhd', raised.astype(jnp.bfloat16), values_part.resha...  21.7 us
  transfers between devices with their start and end apart: 7, of which 5 were waited for; matrix products, arithmetic and copies ran while one was open for 14% of the time, Pallas kernels for 0%

commit v1 on v0

--- a/solution.py
+++ b/solution.py
@@ -85,7 +85,12 @@
     attn = add_rows(attended, lax.all_gather(w_out, "dp", axis=0, tiled=True))
     resid = (local.astype(jnp.float32) + attn).astype(jnp.bfloat16)
     glu_in = layer_norm(resid, ln_conv_gain).astype(jnp.bfloat16)
-    glu_out = add_rows(glu_in, lax.all_gather(w_glu, "dp", axis=0, tiled=True))
+    glu_out = add_rows(
+        glu_in,
+        jnp.concatenate(
+            lax.all_to_all(jnp.stack([w_glu] * lax.axis_size("dp")), "dp", 0, 0), axis=0
+        ),
+    )
     gated = (glu_out[:, :D] * jax.nn.sigmoid(glu_out[:, D:])).astype(jnp.bfloat16)
     half_taps = CONV_K // 2
     widened = with_halo(gated, (("seq", 0),), half_taps)

time: 637 us -> 514 us (0.81)
  waiting for transfers between devices: 472 us -> 316 us
  blocking collectives: 22.1 us -> 34.5 us
  starting transfers between devices: 6.79 us -> 18.9 us
    all_gather x1 -> x0, waiting for transfers between devices: 200 us -> none  [body(): glu_out = add_rows(glu_in, lax.all_gather(w_glu, 'dp', axis=0, tiled=True))]
    all_gather x1, waiting for transfers between devices: 0.02 us -> 53.1 us  [body(): attn = add_rows(attended, lax.all_gather(w_out, 'dp', axis=0, tiled=True))]
    all_gather x1, waiting for transfers between devices: 43.1 us -> 23.7 us  [body(): keys_part = lax.all_gather(keys_local, 'seq', axis=0, tiled=True)]
    all_gather x1, blocking collectives: 22.1 us -> 34.5 us  [body(): all_segs = lax.all_gather(segment_ids, 'seq', axis=1, tiled=True)[0]]
    all_gather x1, waiting for transfers between devices: 61.2 us -> 72.5 us  [body(): values_part = lax.all_gather(values_local, 'seq', axis=0, tiled=True)]
    all_to_all x0 -> x1, starting transfers between devices: none -> 6.99 us  [body(): lax.all_to_all(jnp.stack([w_glu] * lax.axis_size('dp')), 'dp', 0, 0)]
  transfers between devices with their start and end apart: 7 -> 7, of which waited for: 5 -> 5; matrix products, arithmetic and copies ran while one was open for 14% -> 19% of each run, Pallas kernels for 0% -> 0%
where the time goes in v1:
time: 514 us; the launch traced here: 510 us
  waiting for transfers between devices  316 us (61%)
  matrix products  57.8 us (11%)
  other arithmetic  45.1 us (9%)
  blocking collectives  34.5 us (7%)
  local copies, waits for them, and re-layouts  24.2 us (5%)
  starting transfers between devices  18.9 us (4%)
  between operations  13.3 us (3%)
    all_gather x1, waiting for transfers between devices, body(): lax.all_gather(w_qkv, 'dp', axis=0, tiled=True)  159 us
    all_gather x1, waiting for transfers between devices, body(): values_part = lax.all_gather(values_local, 'seq', axis=0, tiled=True)  72.5 us
    all_gather x1, waiting for transfers between devices, body(): attn = add_rows(attended, lax.all_gather(w_out, 'dp', axis=0, tiled=True))  53.1 us
    all_gather x1, blocking collectives, body(): all_segs = lax.all_gather(segment_ids, 'seq', axis=1, tiled=True)[0]  34.5 us
    reduce_sum x1, other arithmetic, body(): totals = jnp.sum(raised, -1)  23.8 us
    all_gather x1, waiting for transfers between devices, body(): keys_part = lax.all_gather(keys_local, 'seq', axis=0, tiled=True)  23.7 us
    dot_general x1, matrix products, body(): jnp.einsum('qhd,khd->hqk', queries, keys_part.reshape(rows, HEADS, HD), p...  23.3 us
    dot_general x1, matrix products, body(): jnp.einsum('hqk,khd->qhd', raised.astype(jnp.bfloat16), values_part.resha...  21.6 us
  transfers between devices with their start and end apart: 7, of which 5 were waited for; matrix products, arithmetic and copies ran while one was open for 19% of the time, Pallas kernels for 0%

profile of v1, /device:TPU:39, one launch (start us, length us, event | category | flops | bytes accessed | tf_op | source)
XLA Modules:
  0.0 510.3 jit_solution(12276052029095379538)
XLA Ops:
  6.5 0.0 copy-start
  6.5 0.0 copy-start.5
  6.5 0.0 all-gather.5.cloned.1.call-start
  6.5 0.7 all-gather.5.cloned.1.call-update
  7.3 0.0 all-gather.9.cloned.1.call-start
  7.3 1.3 convert_reduce_fusion
  8.6 0.0 copy-done
  8.6 0.3 fusion.11
  9.0 159.5 %all-gather.5.cloned.1.call-done = bf16[1536,2304]{1,0:T(8,128)(2,1)} async-done(((bf16[96,2304]{1,0:T(8,128)(2,1)}), bf16[1536,2304]{1,0:T(8,128)(2,1)}) %all-gather.5.cloned.1.call-update) | async-done | bytes 7077904 | tf_op jit(solution)/shard_map/all_gather | solution.py:48
  168.5 0.0 copy-done.5
  168.5 5.1 %convolution_convert_fusion = bf16[256,2304]{1,0:T(8,128)(2,1)S(1)} fusion(bf16[1536,2304]{1,0:T(8,128)(2,1)} %all-gather.5.cloned.1.call-done, bf16[1,256,1536]{2,1,0:T(8,128)(2,1)S(1)} %copy-done, f32[1536]{0:T(1024)S(1)} %copy-done.5, f32[256]{0:T(256)S(1)} %add_rsqrt_fusion.2, f32[256]{0:T(256)S(1)} %broadcast_multiply_fusion.2), kind=kOutput, calls=%fused_computation.36 | convolution fusion | flops 1814495232 | bytes 9052160 | tf_op jit(solution)/shard_map/dot_general | solution.py:34
  173.6 0.0 copy-start.1
  173.6 1.0 fusion.70
  174.6 0.0 all-gather.9.cloned.1.call-update
  174.6 0.0 all-gather.7.cloned.1.call-start
  174.7 0.7 all-gather.7.cloned.1.call-update
  175.3 0.0 copy-done.1
  175.4 4.8 stack.2
  180.1 0.0 copy-start.3
  180.1 0.0 copy-start.2
  180.1 7.0 %all-to-all-start = ((bf16[16,96,3072]{2,1,0:T(8,128)(2,1)}), bf16[16,96,3072]{2,1,0:T(8,128)(2,1)}, u32[]{:S(2)}, u32[]{:S(2)}) async-start(bf16[16,96,3072]{2,1,0:T(8,128)(2,1)} %stack.2), calls=%async_computation | async-start | bytes 18874368 | tf_op jit(solution)/shard_map/all_to_all | solution.py:91
  187.1 0.0 all-gather.11.cloned.1.call-start
  187.1 0.5 all-gather.11.cloned.1.call-update
  187.7 0.0 copy-done.3
  187.7 34.5 %all_gather.19 = s32[1,4096]{1,0:T(1,128)S(1)} all-gather(s32[1,256]{1,0:T(1,128)S(1)} %copy-done.3), channel_id=1, replica_groups=mesh['dp'=16,'seq'=16] {'seq'}, dimensions={1}, use_global_device_ids=true | all-gather | bytes 17408 | tf_op jit(solution)/shard_map/all_gather | solution.py:46
  222.2 0.1 pad_dynamic-slice_fusion
  222.2 0.0 copy-done.2
  222.3 0.3 slice_reduce_fusion.31
  222.6 0.1 slice_compare_fusion.30
  222.7 0.1 slice_compare_fusion.31
  222.8 0.6 broadcast_compare_fusion
  223.4 0.2 copy.14
  223.6 23.7 %all-gather.9.cloned.1.call-done = bf16[4096,768]{1,0:T(8,128)(2,1)} async-done(((bf16[256,768]{1,0:T(8,128)(2,1)}), bf16[4096,768]{1,0:T(8,128)(2,1)}) %all-gather.9.cloned.1.call-update) | async-done | bytes 6291472 | tf_op jit(solution)/shard_map/all_gather | solution.py:54
  247.3 8.6 %copy.15 = bf16[4096,768]{0,1:T(8,128)(2,1)} copy(bf16[4096,768]{1,0:T(8,128)(2,1)} %all-gather.9.cloned.1.call-done) | data formatting | bytes 12582912 | tf_op jit(solution)/shard_map/all_gather | solution.py:54
  255.9 23.3 %fusion = (f32[12,256]{1,0:T(8,128)S(1)}, f32[12,256,4096]{2,1,0:T(8,128)}) fusion(pred[256,4096]{1,0:T(8,128)(4,1)S(1)} %broadcast_compare_fusion, bf16[256,12,64]{0,2,1:T(8,128)(2,1)S(1)} %bitcast.42, bf16[4096,12,64]{0,2,1:T(8,128)(2,1)} %bitcast.40), kind=kOutput, calls=%fused_computation.2 | convolution fusion | flops 1648358400 | bytes 58077184 | tf_op jit(solution)/shard_map/qhd,khd->hqk/dot_general | solution.py:59
  279.2 23.8 %fusion.1 = f32[12,256]{1,0:T(8,128)S(1)} fusion(f32[12,256,4096]{2,1,0:T(8,128)} %get-tuple-element.77, f32[12,256]{1,0:T(8,128)S(1)} %broadcast_maximum_fusion, pred[256,4096]{1,0:T(8,128)(4,1)S(1)} %broadcast_compare_fusion), kind=kLoop, calls=%fused_computation.3 | loop fusion | flops 62911488 | bytes 51404800 | tf_op jit(solution)/shard_map/reduce_sum | solution.py:71
  303.0 72.5 %all-gather.7.cloned.1.call-done = bf16[4096,768]{1,0:T(8,128)(2,1)} async-done(((bf16[256,768]{1,0:T(8,128)(2,1)}), bf16[4096,768]{1,0:T(8,128)(2,1)}) %all-gather.7.cloned.1.call-update) | async-done | bytes 6291472 | tf_op jit(solution)/shard_map/all_gather | solution.py:55
  375.6 8.6 %copy.13 = bf16[4096,768]{0,1:T(8,128)(2,1)} copy(bf16[4096,768]{1,0:T(8,128)(2,1)} %all-gather.7.cloned.1.call-done) | data formatting | bytes 12582912 | tf_op jit(solution)/shard_map/all_gather | solution.py:55
  384.2 21.6 %fusion.25 = bf16[256,12,64]{0,2,1:T(8,128)(2,1)S(1)} fusion(bf16[4096,12,64]{0,2,1:T(8,128)(2,1)} %bitcast.41, f32[12,256,4096]{2,1,0:T(8,128)} %get-tuple-element.77, f32[12,256]{1,0:T(8,128)S(1)} %broadcast_maximum_fusion, pred[256,4096]{1,0:T(8,128)(4,1)S(1)} %broadcast_compare_fusion, f32[256,12]{0,1:T(8,128)S(1)} %bitcast.46), kind=kOutput, calls=%fused_computation.62 | convolution fusion | flops 1673920512 | bytes 58089472 | tf_op jit(solution)/shard_map/hqk,khd->qhd/dot_general | solution.py:72
  405.9 53.1 %all-gather.11.cloned.1.call-done = bf16[768,1536]{1,0:T(8,128)(2,1)} async-done(((bf16[48,1536]{1,0:T(8,128)(2,1)}), bf16[768,1536]{1,0:T(8,128)(2,1)}) %all-gather.11.cloned.1.call-update) | async-done | bytes 2359312 | tf_op jit(solution)/shard_map/all_gather | solution.py:85
  458.9 2.5 fusion.72
  461.5 0.0 copy-start.6
  461.5 0.3 multiply_reduce_fusion.1
  461.8 0.0 all-to-all-done
  461.8 0.4 copy-done.6
  462.2 5.2 %fusion.28 = f32[256,3072]{1,0:T(8,128)S(1)} fusion(bf16[1536,3072]{1,0:T(8,128)(2,1)} %bitcast.9, f32[256,1536]{1,0:T(8,128)S(1)} %get-tuple-element.79, f32[1536]{0:T(1024)S(1)} %copy-done.6, f32[256]{0:T(256)S(1)} %add_rsqrt_fusion.1, f32[256]{0:T(256)S(1)} %broadcast_multiply_fusion.1), kind=kOutput, calls=%fused_computation.63 | convolution fusion | flops 2417491968 | bytes 14163968 | tf_op jit(solution)/shard_map/dot_general | solution.py:34
  467.4 0.4 fusion.18
  467.9 9.9 %collective-permute-start = (bf16[16,1536]{1,0:T(8,128)(2,1)S(1)}, bf16[16,1536]{1,0:T(8,128)(2,1)S(1)}, u32[]{:S(2)}, u32[]{:S(2)}) collective-permute-start(bf16[16,1536]{1,0:T(8,128)(2,1)S(1)} %get-tuple-element.42), channel_id=1, source_target_pairs={{0,1},{1,2},{2,3},{3,4},{4,5},{5,6},{6,7},{7,8},{8,9},{9,10},{10,1... | collective-permute-start | bytes 147464 | tf_op jit(solution)/shard_map/ppermute | solution.py:18
  477.8 1.9 collective-permute-start.1
  479.7 0.2 slice_reduce_fusion.30
  479.9 0.0 collective-permute-done
  479.9 5.7 %collective-permute-done.1 = bf16[16,1536]{1,0:T(8,128)(2,1)S(1)} collective-permute-done((bf16[16,1536]{1,0:T(8,128)(2,1)S(1)}, bf16[16,1536]{1,0:T(8,128)(2,1)S(1)}, u32[]{:S(2)}, u32[]{:S(2)}) %collective-permute-start.1) | collective-permute-done | bytes 49184 | tf_op jit(solution)/shard_map/ppermute | solution.py:21
  485.6 0.0 copy-start.4
  485.6 16.3 %fusion.69 = (f32[256]{0:T(256)S(1)}, f32[256,1536]{1,0:T(8,128)S(1)}) fusion(f32[1536]{0:T(1024)S(1)} %get-tuple-element.35, bf16[16,1536]{1,0:T(8,128)(2,1)S(1)} %collective-permute-done.1, bf16[256,1536]{1,0:T(8,128)(2,1)S(1)} %fusion.18, pred[256]{0:T(512)(128)(4,1)S(1)} %get-tuple-element.45, f32[1536]{0:T(1024)S(1)} %get-tuple-element.36, ...), kind=kLoop, calls=%fused_computation.195 | loop fusion | flops 86900480 | bytes 2663424 | tf_op jit(solution)/shard_map/reduce_sum | solution.py:28
  501.9 0.3 multiply_reduce_fusion
  502.2 0.0 copy-done.4
  502.2 1.5 fusion.65
  (8 shorter events, 0.1 us)
Async XLA Ops:
  6.5 2.1 copy-start
  6.5 161.9 %copy-start.5 = (f32[1536]{0:T(1024)S(1)}, f32[1536]{0:T(1024)}, u32[]{:S(2)}) copy-start(f32[1536]{0:T(1024)} %param.11) | copy-start | bytes 18436
  6.5 161.9 %all-gather.5.cloned.1.call-start = ((), (), s32[]{:S(2)}) async-start(), calls=%async_computation.1 | async-start | bytes 7520256 | tf_op jit(solution)/shard_map/all_gather | solution.py:48
  7.3 240.0 %all-gather.9.cloned.1.call-start = ((), (), s32[]{:S(2)}) async-start(), calls=%async_computation.3 | async-start | bytes 6684672 | tf_op jit(solution)/shard_map/all_gather | solution.py:54
  173.6 1.7 copy-start.1
  174.6 201.0 %all-gather.7.cloned.1.call-start = ((), (), s32[]{:S(2)}) async-start(), calls=%async_computation.2 | async-start | bytes 6684672 | tf_op jit(solution)/shard_map/all_gather | solution.py:55
  180.1 7.6 %copy-start.3 = (s32[1,256]{1,0:T(1,128)S(1)}, s32[1,256]{1,0:T(1,128)}, u32[]{:S(2)}) copy-start(s32[1,256]{1,0:T(1,128)} %param.10) | copy-start | bytes 3076
  180.1 42.1 %copy-start.2 = (f32[32,1536]{1,0:T(8,128)S(1)}, f32[32,1536]{1,0:T(8,128)}, u32[]{:S(2)}) copy-start(f32[32,1536]{1,0:T(8,128)} %param.16) | copy-start | bytes 589828
  180.1 281.7 %all-to-all-start = ((bf16[16,96,3072]{2,1,0:T(8,128)(2,1)}), bf16[16,96,3072]{2,1,0:T(8,128)(2,1)}, u32[]{:S(2)}, u32[]{:S(2)}) async-start(bf16[16,96,3072]{2,1,0:T(8,128)(2,1)} %stack.2), calls=%async_computation | async-start | bytes 18874368 | tf_op jit(solution)/shard_map/all_to_all | solution.py:91
  187.1 271.8 %all-gather.11.cloned.1.call-start = ((), (), s32[]{:S(2)}) async-start(), calls=%async_computation.4 | async-start | bytes 2506752 | tf_op jit(solution)/shard_map/all_gather | solution.py:85
  461.5 0.7 copy-start.6
  467.9 12.1 %collective-permute-start = (bf16[16,1536]{1,0:T(8,128)(2,1)S(1)}, bf16[16,1536]{1,0:T(8,128)(2,1)S(1)}, u32[]{:S(2)}, u32[]{:S(2)}) collective-permute-start(bf16[16,1536]{1,0:T(8,128)(2,1)S(1)} %get-tuple-element.42), channel_id=1, source_target_pairs={{0,1},{1,2},{2,3},{3,4},{4,5},{5,6},{6,7},{7,8},{8,9},{9,10},{10,1... | collective-permute-start | bytes 147464 | tf_op jit(solution)/shard_map/ppermute | solution.py:18
  477.8 7.8 %collective-permute-start.1 = (bf16[16,1536]{1,0:T(8,128)(2,1)S(1)}, bf16[16,1536]{1,0:T(8,128)(2,1)S(1)}, u32[]{:S(2)}, u32[]{:S(2)}) collective-permute-start(bf16[16,1536]{1,0:T(8,128)(2,1)S(1)} %get-tuple-element.43), channel_id=1, source_target_pairs={{1,0},{2,1},{3,2},{4,3},{5,4},{6,5},{7,6},{8,7},{9,8},{10,9},{11,1... | collective-permute-start | bytes 147464 | tf_op jit(solution)/shard_map/ppermute | solution.py:21
  485.6 16.6 %copy-start.4 = (f32[1536]{0:T(1024)S(1)}, f32[1536]{0:T(1024)}, u32[]{:S(2)}) copy-start(f32[1536]{0:T(1024)} %param.17) | copy-start | bytes 18436
Sparse Core Ops, SparseCore 0:
  9.1 159.2 all-gather.4
  174.7 72.5 all-gather.8
  250.1 125.4 all-gather.6
  377.2 81.6 all-gather.10
